TPU v7x, 256 devices: a whole 4x4x8 slice. The times are simulated.
256 devices in a mesh: grp: 2 (over core), dom: 64 (over y_lo, z, x), sub: 2 (over y_hi).
Axes of the slice: x: 4, y: 4 (y_hi: 2, y_lo: 2; y = y_hi * 2 + y_lo), z: 8, core: 2. Of those that a mesh axis runs over, the one named last changes fastest.
Arguments:
- positions: float32 [3, 65536], P(None, ('grp', 'dom', 'sub')), may hold values from 0 to 4
- charges: float32 [65536], P(('grp', 'dom', 'sub')), may hold values from -3 to 3
- polar: float32 [65536], P(('grp', 'dom', 'sub')), may hold values from 0.1 to 0.6
- features: bfloat16 [65536, 256], P(('grp', 'dom', 'sub')), may hold values from -6 to 6
- neighbours: int32 [65536, 32], P(('grp', 'dom', 'sub')), may hold values from 0 to 512, as said below
- send_rows: int32 [2, 32768], P(None, ('grp', 'dom', 'sub')), may hold values from 0 to 255
- blocks: int32 [1024], P(('grp', 'dom', 'sub')), may hold values from 0 to 255
- radial_in: bfloat16 [2, 8, 64], replicated, may hold values from -2 to 2
- radial_mid: bfloat16 [2, 2, 64, 64], replicated, may hold values from -0.75 to 0.75
- radial_out: bfloat16 [2, 64, 256], replicated, may hold values from -0.75 to 0.75
- node_in: bfloat16 [2, 256, 256], replicated, may hold values from -0.375 to 0.375
- node_out: bfloat16 [2, 256, 256], replicated, may hold values from -0.375 to 0.375
- field_gain: float32 [256], replicated, may hold values from -3 to 3
- readout: bfloat16 [256, 2], replicated, may hold values from -0.375 to 0.375
Outputs:
- site_result: float32 [3, 65536], P(None, ('grp', 'dom', 'sub'))
- response: float32 [3, 65536], P(None, ('grp', 'dom', 'sub'))
Inputs may be any that keep to these rules, and one draw needn't show every extreme that they name: `neighbours`: entries below 256 name the block's own sites, entries from 256 to 511 its lent sites, 512 an empty slot; empty slots follow the used ones. `blocks`: repeats may occur.
All inputs are finite; a program needn't handle non-finite values.
Results may differ from a plain program's by a relative error of at most 0.0022.
The roundings to bfloat16 on the way count: a program that leaves them out, or rounds other values in their place, can miss the bound.
Values may be sent and summed in bfloat16 or wider, within the bound.
No kernel may reach another device: no remote copies, remote signals or barrier semaphores. Data moves between devices by JAX's collectives and lax.ppermute only.
A program may use at most 64 MiB of HBM per device.

v0:
```python
import jax
import jax.numpy as jnp
from jax import lax
from jax.sharding import PartitionSpec as P

BASIS = 8
LAYERS = 2
SWEEPS = 4
BLOCK = 128
SMOOTH = 1.0
GAMMA = 1.0
SPACING = 0.75


def with_halo(block, sides, width):
    for axis, dim in sides:
        count = lax.axis_size(axis)
        forward = [(i, i + 1) for i in range(count - 1)]
        backward = [(target, source) for source, target in forward]
        low = lax.ppermute(
            lax.slice_in_dim(block, block.shape[dim] - width, None, axis=dim), axis, forward
        )
        high = lax.ppermute(lax.slice_in_dim(block, 0, width, axis=dim), axis, backward)
        block = jnp.concatenate([low, block, high], axis=dim)
    return block


def partner_2(value, axis, bit):
    mask = 2**bit
    pairs = [(source, source ^ mask) for source in range(lax.axis_size(axis))]
    return lax.ppermute(value, axis, pairs)


def field_at(target, source, charge, dipole):
    tile_count = target.shape[1] // BLOCK
    tiles = target.reshape(3, tile_count, BLOCK).transpose(1, 0, 2)

    def field_one_tile(target_tile):
        offset = target_tile[:, :, None] - source[:, None, :]
        dist_sq = jnp.sum(offset * offset, axis=0) + SMOOTH
        inverse = lax.rsqrt(dist_sq)
        inverse_cube = inverse * inverse * inverse
        inverse_fifth = inverse_cube * inverse * inverse
        projected = jnp.sum(offset * dipole[:, None, :], axis=0)
        source_scale = charge[None, :] * inverse_cube + 3.0 * projected * inverse_fifth
        return jnp.sum(
            offset * source_scale[None] - dipole[:, None, :] * inverse_cube[None], axis=2
        )

    return lax.map(field_one_tile, tiles).transpose(1, 0, 2).reshape(3, -1)


def slot_field(offset, dist_sq, source_charge, source_dipole):
    inverse = lax.rsqrt(dist_sq)
    inverse_cube = inverse * inverse * inverse
    inverse_fifth = inverse_cube * inverse * inverse
    projected = jnp.sum(offset * source_dipole, axis=0)
    source_scale = source_charge * inverse_cube + 3.0 * projected * inverse_fifth
    return jnp.sum(offset * source_scale[None] - source_dipole * inverse_cube[None], axis=1)


def message_update(
    hidden, lifted_table, radial_basis, slot_major, w_first, w_middle, w_last, w_node
):
    row_count, channel_count = hidden.shape
    slot_count = slot_major.shape[0]
    basis_width = radial_basis.shape[2]
    tile_count = row_count // BLOCK

    def message_one_tile(tile_index):
        start = tile_index * BLOCK
        basis_tile = lax.dynamic_slice_in_dim(radial_basis, start, BLOCK, 1).reshape(
            slot_count * BLOCK, basis_width
        )
        index_tile = lax.dynamic_slice_in_dim(slot_major, start, BLOCK, 1)
        first_hidden = jax.nn.silu(
            jnp.dot(basis_tile, w_first, preferred_element_type=jnp.float32)
        ).astype(jnp.bfloat16)
        second_hidden = jax.nn.silu(
            jnp.dot(first_hidden, w_middle[0], preferred_element_type=jnp.float32)
        ).astype(jnp.bfloat16)
        third_hidden = jax.nn.silu(
            jnp.dot(second_hidden, w_middle[1], preferred_element_type=jnp.float32)
        ).astype(jnp.bfloat16)
        edge_weight = jnp.dot(third_hidden, w_last, preferred_element_type=jnp.float32).reshape(
            slot_count, BLOCK, channel_count
        )
        source = lifted_table[index_tile].astype(jnp.float32)
        summed = jnp.sum(edge_weight * source, axis=0)
        return summed / slot_count

    message = (
        lax.map(message_one_tile, jnp.arange(tile_count, dtype=jnp.int32))
        .reshape(row_count, channel_count)
        .astype(jnp.bfloat16)
    )
    update = jax.nn.silu(jnp.dot(message, w_node, preferred_element_type=jnp.float32))
    return (hidden.astype(jnp.float32) + update).astype(jnp.bfloat16)


def extend_cols(values, rim_rows, rim_width):
    empty_entry = jnp.zeros(values.shape[:-1] + (1,), values.dtype)
    return jnp.concatenate(
        [values, rim_rows[..., :rim_width], rim_rows[..., 3 * rim_width :], empty_entry], axis=-1
    )


def extend_rows(values, rim_rows, rim_width):
    empty_entry = jnp.zeros((1,) + values.shape[1:], values.dtype)
    return jnp.concatenate(
        [values, rim_rows[:rim_width], rim_rows[3 * rim_width :], empty_entry], axis=0
    )


def local(
    positions,
    charges,
    polar,
    features,
    neighbours,
    send_rows,
    blocks,
    radial_in,
    radial_mid,
    radial_out,
    node_in,
    node_out,
    field_gain,
    readout,
):
    rim_width = send_rows.shape[1]
    row_count = positions.shape[1]
    block_width = BLOCK
    own_blocks = row_count // block_width
    listed_count = blocks.shape[0]
    domain_count = lax.axis_size(("dom", "sub"))
    domain_index = lax.axis_index(("dom", "sub"))
    group_blocks = own_blocks * domain_count
    learned = lax.axis_index("grp") == 0
    slot_major = neighbours.T
    local_data = jnp.concatenate([positions, charges[None], polar[None]], axis=0)
    outgoing = jnp.concatenate([local_data[:, send_rows[1]], local_data[:, send_rows[0]]], axis=1)
    rim_rows = with_halo(outgoing, ((("dom", "sub"), 1),), rim_width)
    site_table = extend_cols(local_data, rim_rows, rim_width)
    partner = partner_2(local_data, "grp", 0)
    others = lax.all_gather(partner, ("dom", "sub"), axis=1, tiled=True)
    near_sites = jnp.take(others.reshape(5, -1, block_width), blocks, axis=1).reshape(5, -1)
    outside = field_at(positions, near_sites[:3], near_sites[3], jnp.zeros_like(near_sites[:3]))
    offset = positions[:, None, :] - site_table[:3][:, slot_major]
    dist_sq = jnp.sum(offset * offset, axis=0) + SMOOTH
    strength = jnp.sqrt(1.0 + jnp.sum(outside * outside, axis=0))
    hidden = (features.astype(jnp.float32) + strength[:, None] * field_gain[None, :]).astype(
        jnp.bfloat16
    )
    centres = jnp.arange(BASIS, dtype=jnp.float32) * SPACING
    radial_basis = jnp.exp(-GAMMA * (jnp.sqrt(dist_sq)[:, :, None] - centres) ** 2).astype(
        jnp.bfloat16
    )
    for layer_index in range(LAYERS):
        lifted = lax.cond(
            learned,
            lambda h: jnp.dot(h, node_in[layer_index], preferred_element_type=jnp.float32).astype(
                jnp.bfloat16
            ),
            lambda h: jnp.zeros_like(h),
            hidden,
        )
        lent = jnp.concatenate([lifted[send_rows[1]], lifted[send_rows[0]]], axis=0)
        lifted_rims = with_halo(lent, ((("dom", "sub"), 0),), rim_width)
        lifted_table = extend_rows(lifted, lifted_rims, rim_width)
        hidden = lax.cond(
            learned,
            lambda h, t: message_update(
                h,
                t,
                radial_basis,
                slot_major,
                radial_in[layer_index],
                radial_mid[layer_index],
                radial_out[layer_index],
                node_out[layer_index],
            ),
            lambda h, t: h,
            hidden,
            lifted_table,
        )
    readouts = jnp.dot(hidden, readout, preferred_element_type=jnp.float32)
    charge = readouts[:, 0]
    energy = readouts[:, 1]
    fixed_field = outside + slot_field(
        offset, dist_sq, site_table[3][slot_major], jnp.zeros_like(offset)
    )
    dipole = jnp.where(learned, 0.0, polar[None] * fixed_field)
    for sweep_index in range(SWEEPS):
        lent_dipoles = jnp.concatenate([dipole[:, send_rows[1]], dipole[:, send_rows[0]]], axis=1)
        dipole_rims = with_halo(lent_dipoles, ((("dom", "sub"), 1),), rim_width)
        dipole_table = extend_cols(dipole, dipole_rims, rim_width)
        dipole = lax.cond(
            learned,
            lambda d, t: d,
            lambda d, t: polar[None]
            * (
                fixed_field + slot_field(offset, dist_sq, jnp.zeros_like(dist_sq), t[:, slot_major])
            ),
            dipole,
            dipole_table,
        )
    site_result = jnp.where(learned, jnp.stack([charge, energy, strength]), dipole)
    source_charge = jnp.where(learned, charge, 0.0)
    source_dipole = jnp.where(learned, 0.0, dipole)
    response_term = field_at(near_sites[:3], positions, source_charge, source_dipole)
    scattered = (
        jnp.zeros((3, group_blocks, block_width), jnp.float32)
        .at[:, blocks]
        .add(response_term.reshape(3, listed_count, block_width))
        .reshape(3, -1)
    )
    total = lax.psum(scattered, ("dom", "sub"))
    own_share = lax.dynamic_slice_in_dim(total, domain_index * row_count, row_count, 1)
    response = partner_2(own_share, "grp", 0)
    return (site_result, response)


def solution(mesh):
    in_specs = (
        P(None, ("grp", "dom", "sub")),
        P(("grp", "dom", "sub")),
        P(("grp", "dom", "sub")),
        P(("grp", "dom", "sub"), None),
        P(("grp", "dom", "sub"), None),
        P(None, ("grp", "dom", "sub")),
        P(("grp", "dom", "sub")),
        P(),
        P(),
        P(),
        P(),
        P(),
        P(),
        P(),
    )
    out_specs = (P(None, ("grp", "dom", "sub")), P(None, ("grp", "dom", "sub")))
    return jax.shard_map(local, mesh=mesh, in_specs=in_specs, out_specs=out_specs, check_vma=False)
```

profile of v0, /device:TPU:1, one launch (start us, length us, event | category | flops | bytes accessed | tf_op | source)
XLA Modules:
  0.0 878.2 jit_solution(3538958461297963734)
XLA Ops:
  14.7 5.5 collective-permute-start.1
  24.2 32.9 %gather_fusion.14 = f32[8192]{0:T(1024)S(1)} fusion(f32[513]{0:T(1024)S(1)} %slice_reduce_fusion, s32[8192]{0:T(1024)S(1)} %broadcast_clamp_fusion.4), kind=kCustom, calls=%fused_computation.14 | custom fusion | bytes 98304 | tf_op jit(solution)/shard_map/gather | solution.py:191
  57.2 27.9 %gather_fusion.9 = f32[8192,3]{1,0:T(8,128)} fusion(f32[3,513]{0,1:T(8,128)S(1)} %copy.124, s32[8192]{0:T(1024)S(1)} %broadcast_clamp_fusion.4), kind=kCustom, calls=%fused_computation.9 | custom fusion | bytes 229376 | tf_op jit(solution)/shard_map/gather | solution.py:149
  94.0 296.4 %all_gather.3 = f32[5,32768]{1,0:T(8,128)S(1)} all-gather(f32[5,256]{1,0:T(8,128)S(1)} %collective-permute-done), channel_id=1, replica_groups=mesh['grp'=2,'dom'=64,'sub'=2] {'dom','sub'}, dimensions={1}, use_global_device_ids=true | all-gather | bytes 660480 | tf_op jit(solution)/shard_map/all_gather | solution.py:146
  395.2 5.5 collective-permute-start.7
  402.1 36.6 %conditional.12 = (f32[3,256]{0,1:T(8,128)S(1)}) conditional(s32[]{:T(128)} %convert_element_type.76, (f32[256]{0:T(256)S(1)}, f32[32,256]{1,0:T(8,128)S(1)}, s32[32,256]{1,0:T(8,128)S(1)}, f32[3,513]{1,0:T(4,128)S(1)}, f32[3,32,256]{0,2,1:T(8,128)}, /*index=5*/f32[3,256]{0,1:T(8,128)S(1)}) %tuple.225, f32[3,256]{0,1:T(8,128)S(1)} %get-tuple-element.543), branch_computations={%region_23.26_spmd, %region_26.27_spmd} | conditional | flops 238336 | bytes 1860696 | solution.py:198
  402.3 27.9 %gather_fusion = f32[8192,3]{1,0:T(8,128)} fusion(f32[3,513]{0,1:T(8,128)S(1)} %copy.129, s32[8192]{0:T(1024)S(1)} %broadcast_clamp_fusion), kind=kCustom, calls=%fused_computation.2 | custom fusion | bytes 229376 | tf_op jit(solution)/shard_map/cond/branch_0_fun/gather | solution.py:203
  430.2 4.8 multiply_reduce_fusion
  441.3 6.1 collective-permute-start.9
  448.9 36.7 %conditional.13 = (f32[3,256]{0,1:T(8,128)S(1)}) conditional(s32[]{:T(128)} %convert_element_type.76, (f32[256]{0:T(256)S(1)}, f32[32,256]{1,0:T(8,128)S(1)}, s32[32,256]{1,0:T(8,128)S(1)}, f32[3,513]{1,0:T(4,128)S(1)}, f32[3,32,256]{0,2,1:T(8,128)}, /*index=5*/f32[3,256]{0,1:T(8,128)S(1)}) %tuple.226, f32[3,256]{0,1:T(8,128)S(1)} %get-tuple-element.898), branch_computations={%region_27.30_spmd, %region_30.31_spmd} | conditional | flops 238336 | bytes 1860696 | solution.py:198
  449.1 27.9 %gather_fusion.1 = f32[8192,3]{1,0:T(8,128)} fusion(f32[3,513]{0,1:T(8,128)S(1)} %copy.133, s32[8192]{0:T(1024)S(1)} %broadcast_clamp_fusion.1), kind=kCustom, calls=%fused_computation.3 | custom fusion | bytes 229376 | tf_op jit(solution)/shard_map/cond/branch_0_fun/gather | solution.py:203
  477.0 4.8 multiply_reduce_fusion.1
  488.1 6.4 collective-permute-start.11
  497.9 6.7 collective-permute-start.3
  504.9 36.6 %conditional.14 = (f32[3,256]{0,1:T(8,128)S(1)}) conditional(s32[]{:T(128)} %convert_element_type.76, (f32[256]{0:T(256)S(1)}, f32[32,256]{1,0:T(8,128)S(1)}, s32[32,256]{1,0:T(8,128)S(1)}, f32[3,513]{1,0:T(4,128)S(1)}, f32[3,32,256]{0,2,1:T(8,128)}, /*index=5*/f32[3,256]{0,1:T(8,128)S(1)}) %tuple.227, f32[3,256]{0,1:T(8,128)S(1)} %get-tuple-element.899), branch_computations={%region_31.34_spmd, %region_34.35_spmd} | conditional | flops 238336 | bytes 1860696 | solution.py:198
  505.1 27.9 %gather_fusion.2 = f32[8192,3]{1,0:T(8,128)} fusion(f32[3,513]{0,1:T(8,128)S(1)} %copy.137, s32[8192]{0:T(1024)S(1)} %broadcast_clamp_fusion.2), kind=kCustom, calls=%fused_computation.4 | custom fusion | bytes 229376 | tf_op jit(solution)/shard_map/cond/branch_0_fun/gather | solution.py:203
  533.0 4.8 multiply_reduce_fusion.2
  544.1 6.4 collective-permute-start.13
  555.2 6.4 collective-permute-start.5
  561.6 36.6 %conditional.15 = (f32[3,256]{0,1:T(8,128)S(1)}) conditional(s32[]{:T(128)} %convert_element_type.76, (f32[256]{0:T(256)S(1)}, f32[32,256]{1,0:T(8,128)S(1)}, s32[32,256]{1,0:T(8,128)S(1)}, f32[3,513]{1,0:T(4,128)S(1)}, f32[3,32,256]{0,2,1:T(8,128)}, /*index=5*/f32[3,256]{0,1:T(8,128)S(1)}) %tuple.228, f32[3,256]{0,1:T(8,128)S(1)} %get-tuple-element.900), branch_computations={%region_35.38_spmd, %region_38.39_spmd} | conditional | flops 238336 | bytes 1860696 | solution.py:198
  561.8 27.9 %gather_fusion.3 = f32[8192,3]{1,0:T(8,128)} fusion(f32[3,513]{0,1:T(8,128)S(1)} %copy.141, s32[8192]{0:T(1024)S(1)} %broadcast_clamp_fusion.3), kind=kCustom, calls=%fused_computation.5 | custom fusion | bytes 229376 | tf_op jit(solution)/shard_map/cond/branch_0_fun/gather | solution.py:203
  589.7 4.8 multiply_reduce_fusion.3
  602.6 261.5 %all-reduce.2.cloned.1.call-done = f32[3,32768]{1,0:T(4,128)} async-done(((f32[3,32768]{1,0:T(4,128)}), f32[3,32768]{1,0:T(4,128)}) %all-reduce.2.cloned.1.call-update) | async-done | bytes 393232 | tf_op jit(solution)/shard_map/psum | solution.py:218
  864.8 5.2 collective-permute-start.15
  (218 shorter events, 68.6 us)
Async XLA Ops:
  7.2 591.5 %copy-start = (bf16[256,2]{0,1:T(2,128)(2,1)S(1)}, bf16[256,2]{0,1:T(2,128)(2,1)}, u32[]{:S(2)}) copy-start(bf16[256,2]{0,1:T(2,128)(2,1)} %param.51) | copy-start | bytes 3076
  7.2 856.9 %all-reduce.2.cloned.1.call-start = ((), (), s32[]{:S(2)}) async-start(), calls=%async_computation | async-start | bytes 1048576 | tf_op jit(solution)/shard_map/psum | solution.py:218
  8.0 86.1 %collective-permute-start = (f32[5,256]{1,0:T(8,128)S(1)}, f32[5,256]{1,0:T(8,128)S(1)}, u32[]{:S(2)}, u32[]{:S(2)}) collective-permute-start(f32[5,256]{1,0:T(8,128)S(1)} %pad_maximum_fusion), channel_id=1, source_target_pairs={{0,128},{128,0},{1,129},{129,1},{2,130},{130,2},{3,131},{131,3},{4... | collective-permute-start | bytes 15368 | tf_op jit(solution)/shard_map/ppermute | solution.py:31
  12.8 10.5 %collective-permute-start.2 = (f32[5,128]{0,1:T(8,128)S(1)}, f32[5,128]{0,1:T(8,128)S(1)}, u32[]{:S(2)}, u32[]{:S(2)}) collective-permute-start(f32[5,128]{0,1:T(8,128)S(1)} %bitcast.260), channel_id=1, source_target_pairs={{1,0},{2,1},{3,2},{4,3},{5,4},{6,5},{7,6},{8,7},{9,8},{10,9},{11,1... | collective-permute-start | bytes 7688 | tf_op jit(solution)/shard_map/ppermute | solution.py:23
  14.7 8.6 collective-permute-start.1
  89.6 301.4 %copy-start.12 = (f32[3,256]{1,0:T(4,128)S(1)}, f32[3,256]{1,0:T(4,128)}, u32[]{:S(2)}) copy-start(f32[3,256]{1,0:T(4,128)} %param.38) | copy-start | bytes 9220
  393.9 6.9 collective-permute-start.8
  395.2 6.8 collective-permute-start.7
  440.0 7.5 collective-permute-start.10
  441.3 7.4 collective-permute-start.9
  448.8 45.7 %copy-start.14 = (bf16[256,256]{1,0:T(8,128)(2,1)S(1)}, bf16[256,256]{1,0:T(8,128)(2,1)}, u32[]{:S(2)}) copy-start(bf16[256,256]{1,0:T(8,128)(2,1)} %param.41) | copy-start | bytes 393220
  448.8 45.8 %copy-start.13 = (bf16[2,256,256]{2,1,0:T(8,128)(2,1)S(1)}, bf16[2,256,256]{2,1,0:T(8,128)(2,1)}, u32[]{:S(2)}) copy-start(bf16[2,256,256]{2,1,0:T(8,128)(2,1)} %param.48) | copy-start | bytes 786436
  486.8 17.9 %collective-permute-start.12 = (f32[3,128]{0,1:T(8,128)S(1)}, f32[3,128]{0,1:T(8,128)S(1)}, u32[]{:S(2)}, u32[]{:S(2)}) collective-permute-start(f32[3,128]{0,1:T(8,128)S(1)} %bitcast.263), channel_id=1, source_target_pairs={{1,0},{2,1},{3,2},{4,3},{5,4},{6,5},{7,6},{8,7},{9,8},{10,9},{11,1... | collective-permute-start | bytes 4616 | tf_op jit(solution)/shard_map/ppermute | solution.py:23
  488.1 16.7 %collective-permute-start.11 = (f32[3,128]{0,1:T(8,128)S(1)}, f32[3,128]{0,1:T(8,128)S(1)}, u32[]{:S(2)}, u32[]{:S(2)}) collective-permute-start(f32[3,128]{0,1:T(8,128)S(1)} %bitcast.262), channel_id=1, source_target_pairs={{0,1},{1,2},{2,3},{3,4},{4,5},{5,6},{6,7},{7,8},{8,9},{9,10},{10,1... | collective-permute-start | bytes 4616 | tf_op jit(solution)/shard_map/ppermute | solution.py:20
  496.6 55.3 %collective-permute-start.4 = (bf16[128,256]{1,0:T(8,128)(2,1)S(1)}, bf16[128,256]{1,0:T(8,128)(2,1)S(1)}, u32[]{:S(2)}, u32[]{:S(2)}) collective-permute-start(bf16[128,256]{1,0:T(8,128)(2,1)S(1)} %gather_fusion.11), channel_id=1, source_target_pairs={{1,0},{2,1},{3,2},{4,3},{5,4},{6,5},{7,6},{8,7},{9,8},{10,9},{11,1... | collective-permute-start | bytes 196616 | tf_op jit(solution)/shard_map/ppermute | solution.py:23
  497.9 54.0 %collective-permute-start.3 = (bf16[128,256]{1,0:T(8,128)(2,1)S(1)}, bf16[128,256]{1,0:T(8,128)(2,1)S(1)}, u32[]{:S(2)}, u32[]{:S(2)}) collective-permute-start(bf16[128,256]{1,0:T(8,128)(2,1)S(1)} %gather_fusion.10), channel_id=1, source_target_pairs={{0,1},{1,2},{2,3},{3,4},{4,5},{5,6},{6,7},{7,8},{8,9},{9,10},{10,1... | collective-permute-start | bytes 196616 | tf_op jit(solution)/shard_map/ppermute | solution.py:20
  504.9 47.2 %copy-start.15 = (bf16[2,2,64,64]{3,2,1,0:T(8,128)(2,1)S(1)}, bf16[2,2,64,64]{3,2,1,0:T(8,128)(2,1)}, u32[]{:S(2)}) copy-start(bf16[2,2,64,64]{3,2,1,0:T(8,128)(2,1)} %param.46) | copy-start | bytes 98308
  504.9 47.2 %copy-start.16 = (bf16[2,64,256]{2,1,0:T(8,128)(2,1)S(1)}, bf16[2,64,256]{2,1,0:T(8,128)(2,1)}, u32[]{:S(2)}) copy-start(bf16[2,64,256]{2,1,0:T(8,128)(2,1)} %param.47) | copy-start | bytes 196612
  504.9 47.2 %copy-start.19 = (bf16[2,8,64]{2,1,0:T(8,128)(2,1)S(1)}, bf16[2,8,64]{2,1,0:T(8,128)(2,1)}, u32[]{:S(2)}) copy-start(bf16[2,8,64]{2,1,0:T(8,128)(2,1)} %param.45) | copy-start | bytes 6148
  542.8 7.9 collective-permute-start.14
  544.1 7.7 collective-permute-start.13
  553.9 44.4 %collective-permute-start.6 = (bf16[128,256]{1,0:T(8,128)(2,1)S(1)}, bf16[128,256]{1,0:T(8,128)(2,1)S(1)}, u32[]{:S(2)}, u32[]{:S(2)}) collective-permute-start(bf16[128,256]{1,0:T(8,128)(2,1)S(1)} %gather_fusion.13), channel_id=1, source_target_pairs={{1,0},{2,1},{3,2},{4,3},{5,4},{6,5},{7,6},{8,7},{9,8},{10,9},{11,1... | collective-permute-start | bytes 196616 | tf_op jit(solution)/shard_map/ppermute | solution.py:23
  555.2 43.1 %collective-permute-start.5 = (bf16[128,256]{1,0:T(8,128)(2,1)S(1)}, bf16[128,256]{1,0:T(8,128)(2,1)S(1)}, u32[]{:S(2)}, u32[]{:S(2)}) collective-permute-start(bf16[128,256]{1,0:T(8,128)(2,1)S(1)} %gather_fusion.12), channel_id=1, source_target_pairs={{0,1},{1,2},{2,3},{3,4},{4,5},{5,6},{6,7},{7,8},{8,9},{9,10},{10,1... | collective-permute-start | bytes 196616 | tf_op jit(solution)/shard_map/ppermute | solution.py:20
  864.8 6.0 collective-permute-start.15
  (16 other events, 109.3 us)
Sparse Core Ops, SparseCore 0:
  602.7 261.3 all-reduce.1
where the time goes:
time: 879 us; the launch traced here: 878 us
  blocking collectives  296 us (34%)
  waiting for transfers between devices  265 us (30%)
  local copies, waits for them, and re-layouts  195 us (22%)
  starting transfers between devices  60.5 us (7%)
  other arithmetic  45.1 us (5%)
  between operations  14.8 us (2%)
    all_gather x1, blocking collectives, local(): others = lax.all_gather(partner, ('dom', 'sub'), axis=1, tiled=True)  296 us
    psum x1, waiting for transfers between devices, local(): total = lax.psum(scattered, ('dom', 'sub'))  262 us
    gather x4, local copies, waits for them, and re-layouts, local(): t[:, slot_major]  112 us
    ppermute x7, starting transfers between devices, with_halo(): lax.ppermute(lax.slice_in_dim(block, block.shape[dim] - width, None, axis...  43 us
    gather x2, local copies, waits for them, and re-layouts, local(): site_table[3][slot_major]  32.9 us
    gather x1, local copies, waits for them, and re-layouts, local(): offset = positions[:, None, :] - site_table[:3][:, slot_major]  27.9 us
    reduce_sum x5, other arithmetic, slot_field(): projected = jnp.sum(offset * source_dipole, axis=0)  23.5 us
  transfers between devices with their start and end apart: 17, of which 5 were waited for; matrix products, arithmetic and copies ran while one was open for 17% of the time, Pallas kernels for 0%

commit v1 on v0

--- a/solution.py
+++ b/solution.py
@@ -215,7 +215,7 @@
         .add(response_term.reshape(3, listed_count, block_width))
         .reshape(3, -1)
     )
-    total = lax.psum(scattered, ("dom", "sub"))
+    total = lax.psum(lax.psum(scattered, "sub"), "dom")
     own_share = lax.dynamic_slice_in_dim(total, domain_index * row_count, row_count, 1)
     response = partner_2(own_share, "grp", 0)
     return (site_result, response)

time: 879 us -> 1310 us (1.49)
  waiting for transfers between devices: 265 us -> 656 us
  starting transfers between devices: 60.5 us -> 98.6 us
    psum x1 -> x2, waiting for transfers between devices: 262 us -> 652 us  [local(): total = lax.psum(lax.psum(scattered, 'sub'), 'dom')]
    ppermute x2, starting transfers between devices: 8.43 us -> 46.5 us  [partner_2(): return lax.ppermute(value, axis, pairs)]
  transfers between devices with their start and end apart: 17 -> 18, of which waited for: 5 -> 6; matrix products, arithmetic and copies ran while one was open for 17% -> 11% of each run, Pallas kernels for 0% -> 0%
where the time goes in v1:
time: 1310 us
  waiting for transfers between devices  656 us (50%)
  blocking collectives  296 us (23%)
  local copies, waits for them, and re-layouts  195 us (15%)
  starting transfers between devices  98.6 us (8%)
  other arithmetic  45.1 us (3%)
  between operations  14.8 us (1%)
    psum x2, waiting for transfers between devices, local(): total = lax.psum(lax.psum(scattered, 'sub'), 'dom')  652 us
    all_gather x1, blocking collectives, local(): others = lax.all_gather(partner, ('dom', 'sub'), axis=1, tiled=True)  296 us
    gather x4, local copies, waits for them, and re-layouts, local(): t[:, slot_major]  112 us
    ppermute x2, starting transfers between devices, partner_2(): return lax.ppermute(value, axis, pairs)  46.5 us
    ppermute x7, starting transfers between devices, with_halo(): lax.ppermute(lax.slice_in_dim(block, block.shape[dim] - width, None, axis...  43 us
    gather x2, local copies, waits for them, and re-layouts, local(): site_table[3][slot_major]  32.9 us
    gather x1, local copies, waits for them, and re-layouts, local(): offset = positions[:, None, :] - site_table[:3][:, slot_major]  27.9 us
  transfers between devices with their start and end apart: 18, of which 6 were waited for; matrix products, arithmetic and copies ran while one was open for 11% of the time, Pallas kernels for 0%

profile of v1, /device:TPU:1, one launch (start us, length us, event | category | flops | bytes accessed | tf_op | source)
XLA Modules:
  0.0 1307.1 jit_solution(15734483733312606255)
XLA Ops:
  14.7 5.5 collective-permute-start.1
  24.2 32.9 %gather_fusion.14 = f32[8192]{0:T(1024)S(1)} fusion(f32[513]{0:T(1024)S(1)} %slice_reduce_fusion, s32[8192]{0:T(1024)S(1)} %broadcast_clamp_fusion.4), kind=kCustom, calls=%fused_computation.14 | custom fusion | bytes 98304 | tf_op jit(solution)/shard_map/gather | solution.py:191
  57.2 27.9 %gather_fusion.9 = f32[8192,3]{1,0:T(8,128)} fusion(f32[3,513]{0,1:T(8,128)S(1)} %copy.124, s32[8192]{0:T(1024)S(1)} %broadcast_clamp_fusion.4), kind=kCustom, calls=%fused_computation.9 | custom fusion | bytes 229376 | tf_op jit(solution)/shard_map/gather | solution.py:149
  94.0 296.4 %all_gather.3 = f32[5,32768]{1,0:T(8,128)S(1)} all-gather(f32[5,256]{1,0:T(8,128)S(1)} %collective-permute-done), channel_id=1, replica_groups=mesh['grp'=2,'dom'=64,'sub'=2] {'dom','sub'}, dimensions={1}, use_global_device_ids=true | all-gather | bytes 660480 | tf_op jit(solution)/shard_map/all_gather | solution.py:146
  395.2 5.5 collective-permute-start.7
  402.1 36.6 %conditional.12 = (f32[3,256]{0,1:T(8,128)S(1)}) conditional(s32[]{:T(128)} %convert_element_type.76, (f32[256]{0:T(256)S(1)}, f32[32,256]{1,0:T(8,128)S(1)}, s32[32,256]{1,0:T(8,128)S(1)}, f32[3,513]{1,0:T(4,128)S(1)}, f32[3,32,256]{0,2,1:T(8,128)}, /*index=5*/f32[3,256]{0,1:T(8,128)S(1)}) %tuple.227, f32[3,256]{0,1:T(8,128)S(1)} %get-tuple-element.543), branch_computations={%region_23.26_spmd, %region_26.27_spmd} | conditional | flops 238336 | bytes 1860696 | solution.py:198
  402.3 27.9 %gather_fusion = f32[8192,3]{1,0:T(8,128)} fusion(f32[3,513]{0,1:T(8,128)S(1)} %copy.129, s32[8192]{0:T(1024)S(1)} %broadcast_clamp_fusion), kind=kCustom, calls=%fused_computation.2 | custom fusion | bytes 229376 | tf_op jit(solution)/shard_map/cond/branch_0_fun/gather | solution.py:203
  430.2 4.8 multiply_reduce_fusion
  441.3 6.1 collective-permute-start.9
  448.9 36.7 %conditional.13 = (f32[3,256]{0,1:T(8,128)S(1)}) conditional(s32[]{:T(128)} %convert_element_type.76, (f32[256]{0:T(256)S(1)}, f32[32,256]{1,0:T(8,128)S(1)}, s32[32,256]{1,0:T(8,128)S(1)}, f32[3,513]{1,0:T(4,128)S(1)}, f32[3,32,256]{0,2,1:T(8,128)}, /*index=5*/f32[3,256]{0,1:T(8,128)S(1)}) %tuple.228, f32[3,256]{0,1:T(8,128)S(1)} %get-tuple-element.898), branch_computations={%region_27.30_spmd, %region_30.31_spmd} | conditional | flops 238336 | bytes 1860696 | solution.py:198
  449.1 27.9 %gather_fusion.1 = f32[8192,3]{1,0:T(8,128)} fusion(f32[3,513]{0,1:T(8,128)S(1)} %copy.133, s32[8192]{0:T(1024)S(1)} %broadcast_clamp_fusion.1), kind=kCustom, calls=%fused_computation.3 | custom fusion | bytes 229376 | tf_op jit(solution)/shard_map/cond/branch_0_fun/gather | solution.py:203
  477.0 4.8 multiply_reduce_fusion.1
  488.1 6.4 collective-permute-start.11
  497.9 6.7 collective-permute-start.3
  504.9 36.6 %conditional.14 = (f32[3,256]{0,1:T(8,128)S(1)}) conditional(s32[]{:T(128)} %convert_element_type.76, (f32[256]{0:T(256)S(1)}, f32[32,256]{1,0:T(8,128)S(1)}, s32[32,256]{1,0:T(8,128)S(1)}, f32[3,513]{1,0:T(4,128)S(1)}, f32[3,32,256]{0,2,1:T(8,128)}, /*index=5*/f32[3,256]{0,1:T(8,128)S(1)}) %tuple.229, f32[3,256]{0,1:T(8,128)S(1)} %get-tuple-element.899), branch_computations={%region_31.34_spmd, %region_34.35_spmd} | conditional | flops 238336 | bytes 1860696 | solution.py:198
  505.1 27.9 %gather_fusion.2 = f32[8192,3]{1,0:T(8,128)} fusion(f32[3,513]{0,1:T(8,128)S(1)} %copy.137, s32[8192]{0:T(1024)S(1)} %broadcast_clamp_fusion.2), kind=kCustom, calls=%fused_computation.4 | custom fusion | bytes 229376 | tf_op jit(solution)/shard_map/cond/branch_0_fun/gather | solution.py:203
  533.0 4.8 multiply_reduce_fusion.2
  544.1 6.4 collective-permute-start.13
  555.2 6.4 collective-permute-start.5
  561.6 36.6 %conditional.15 = (f32[3,256]{0,1:T(8,128)S(1)}) conditional(s32[]{:T(128)} %convert_element_type.76, (f32[256]{0:T(256)S(1)}, f32[32,256]{1,0:T(8,128)S(1)}, s32[32,256]{1,0:T(8,128)S(1)}, f32[3,513]{1,0:T(4,128)S(1)}, f32[3,32,256]{0,2,1:T(8,128)}, /*index=5*/f32[3,256]{0,1:T(8,128)S(1)}) %tuple.230, f32[3,256]{0,1:T(8,128)S(1)} %get-tuple-element.900), branch_computations={%region_35.38_spmd, %region_38.39_spmd} | conditional | flops 238336 | bytes 1860696 | solution.py:198
  561.8 27.9 %gather_fusion.3 = f32[8192,3]{1,0:T(8,128)} fusion(f32[3,513]{0,1:T(8,128)S(1)} %copy.141, s32[8192]{0:T(1024)S(1)} %broadcast_clamp_fusion.3), kind=kCustom, calls=%fused_computation.5 | custom fusion | bytes 229376 | tf_op jit(solution)/shard_map/cond/branch_0_fun/gather | solution.py:203
  602.6 91.5 %all-reduce.3.cloned.1.call-done = f32[3,32768]{1,0:T(4,128)} async-done(((f32[3,32768]{1,0:T(4,128)}), f32[3,32768]{1,0:T(4,128)}) %all-reduce.3.cloned.1.call-update) | async-done | bytes 393232 | tf_op jit(solution)/shard_map/psum | solution.py:218
  694.1 560.8 %all-reduce.5.cloned.1.call-done = f32[3,32768]{1,0:T(4,128)} async-done(((f32[3,32768]{1,0:T(4,128)}), f32[3,32768]{1,0:T(4,128)}) %all-reduce.5.cloned.1.call-update) | async-done | bytes 393232 | tf_op jit(solution)/shard_map/psum | solution.py:218
  1255.6 43.3 %collective-permute-start.15 = (f32[3,256]{1,0:T(4,128)S(1)}, f32[3,256]{1,0:T(4,128)S(1)}, u32[]{:S(2)}, u32[]{:S(2)}) collective-permute-start(f32[3,256]{1,0:T(4,128)S(1)} %constant_dynamic-slice_fusion), channel_id=1, source_target_pairs={{0,128},{128,0},{1,129},{129,1},{2,130},{130,2},{3,131},{131,3},{4... | collective-permute-start | bytes 9224 | tf_op jit(solution)/shard_map/ppermute | solution.py:31
  (221 shorter events, 73.4 us)
Async XLA Ops:
  7.2 591.5 %copy-start = (bf16[256,2]{0,1:T(2,128)(2,1)S(1)}, bf16[256,2]{0,1:T(2,128)(2,1)}, u32[]{:S(2)}) copy-start(bf16[256,2]{0,1:T(2,128)(2,1)} %param.51) | copy-start | bytes 3076
  7.2 686.9 %all-reduce.3.cloned.1.call-start = ((), (), s32[]{:S(2)}) async-start(), calls=%async_computation | async-start | bytes 1048576 | tf_op jit(solution)/shard_map/psum | solution.py:218
  8.0 86.1 %collective-permute-start = (f32[5,256]{1,0:T(8,128)S(1)}, f32[5,256]{1,0:T(8,128)S(1)}, u32[]{:S(2)}, u32[]{:S(2)}) collective-permute-start(f32[5,256]{1,0:T(8,128)S(1)} %pad_maximum_fusion), channel_id=1, source_target_pairs={{0,128},{128,0},{1,129},{129,1},{2,130},{130,2},{3,131},{131,3},{4... | collective-permute-start | bytes 15368 | tf_op jit(solution)/shard_map/ppermute | solution.py:31
  12.8 10.5 collective-permute-start.2
  14.7 8.6 collective-permute-start.1
  89.6 301.4 %copy-start.12 = (f32[3,256]{1,0:T(4,128)S(1)}, f32[3,256]{1,0:T(4,128)}, u32[]{:S(2)}) copy-start(f32[3,256]{1,0:T(4,128)} %param.38) | copy-start | bytes 9220
  393.9 6.9 collective-permute-start.8
  395.2 6.8 collective-permute-start.7
  440.0 7.5 collective-permute-start.10
  441.3 7.4 collective-permute-start.9
  448.8 45.8 %copy-start.13 = (bf16[2,256,256]{2,1,0:T(8,128)(2,1)S(1)}, bf16[2,256,256]{2,1,0:T(8,128)(2,1)}, u32[]{:S(2)}) copy-start(bf16[2,256,256]{2,1,0:T(8,128)(2,1)} %param.48) | copy-start | bytes 786436
  486.8 17.9 %collective-permute-start.12 = (f32[3,128]{0,1:T(8,128)S(1)}, f32[3,128]{0,1:T(8,128)S(1)}, u32[]{:S(2)}, u32[]{:S(2)}) collective-permute-start(f32[3,128]{0,1:T(8,128)S(1)} %bitcast.263), channel_id=1, source_target_pairs={{1,0},{2,1},{3,2},{4,3},{5,4},{6,5},{7,6},{8,7},{9,8},{10,9},{11,1... | collective-permute-start | bytes 4616 | tf_op jit(solution)/shard_map/ppermute | solution.py:23
  488.1 16.7 %collective-permute-start.11 = (f32[3,128]{0,1:T(8,128)S(1)}, f32[3,128]{0,1:T(8,128)S(1)}, u32[]{:S(2)}, u32[]{:S(2)}) collective-permute-start(f32[3,128]{0,1:T(8,128)S(1)} %bitcast.262), channel_id=1, source_target_pairs={{0,1},{1,2},{2,3},{3,4},{4,5},{5,6},{6,7},{7,8},{8,9},{9,10},{10,1... | collective-permute-start | bytes 4616 | tf_op jit(solution)/shard_map/ppermute | solution.py:20
  496.6 55.3 %collective-permute-start.4 = (bf16[128,256]{1,0:T(8,128)(2,1)S(1)}, bf16[128,256]{1,0:T(8,128)(2,1)S(1)}, u32[]{:S(2)}, u32[]{:S(2)}) collective-permute-start(bf16[128,256]{1,0:T(8,128)(2,1)S(1)} %gather_fusion.11), channel_id=1, source_target_pairs={{1,0},{2,1},{3,2},{4,3},{5,4},{6,5},{7,6},{8,7},{9,8},{10,9},{11,1... | collective-permute-start | bytes 196616 | tf_op jit(solution)/shard_map/ppermute | solution.py:23
  497.9 54.0 %collective-permute-start.3 = (bf16[128,256]{1,0:T(8,128)(2,1)S(1)}, bf16[128,256]{1,0:T(8,128)(2,1)S(1)}, u32[]{:S(2)}, u32[]{:S(2)}) collective-permute-start(bf16[128,256]{1,0:T(8,128)(2,1)S(1)} %gather_fusion.10), channel_id=1, source_target_pairs={{0,1},{1,2},{2,3},{3,4},{4,5},{5,6},{6,7},{7,8},{8,9},{9,10},{10,1... | collective-permute-start | bytes 196616 | tf_op jit(solution)/shard_map/ppermute | solution.py:20
  504.9 47.2 %copy-start.15 = (bf16[2,2,64,64]{3,2,1,0:T(8,128)(2,1)S(1)}, bf16[2,2,64,64]{3,2,1,0:T(8,128)(2,1)}, u32[]{:S(2)}) copy-start(bf16[2,2,64,64]{3,2,1,0:T(8,128)(2,1)} %param.46) | copy-start | bytes 98308
  504.9 47.2 %copy-start.16 = (bf16[2,64,256]{2,1,0:T(8,128)(2,1)S(1)}, bf16[2,64,256]{2,1,0:T(8,128)(2,1)}, u32[]{:S(2)}) copy-start(bf16[2,64,256]{2,1,0:T(8,128)(2,1)} %param.47) | copy-start | bytes 196612
  504.9 47.2 %copy-start.19 = (bf16[2,8,64]{2,1,0:T(8,128)(2,1)S(1)}, bf16[2,8,64]{2,1,0:T(8,128)(2,1)}, u32[]{:S(2)}) copy-start(bf16[2,8,64]{2,1,0:T(8,128)(2,1)} %param.45) | copy-start | bytes 6148
  542.8 7.9 collective-permute-start.14
  544.1 7.7 collective-permute-start.13
  553.9 44.4 %collective-permute-start.6 = (bf16[128,256]{1,0:T(8,128)(2,1)S(1)}, bf16[128,256]{1,0:T(8,128)(2,1)S(1)}, u32[]{:S(2)}, u32[]{:S(2)}) collective-permute-start(bf16[128,256]{1,0:T(8,128)(2,1)S(1)} %gather_fusion.13), channel_id=1, source_target_pairs={{1,0},{2,1},{3,2},{4,3},{5,4},{6,5},{7,6},{8,7},{9,8},{10,9},{11,1... | collective-permute-start | bytes 196616 | tf_op jit(solution)/shard_map/ppermute | solution.py:23
  555.2 43.1 %collective-permute-start.5 = (bf16[128,256]{1,0:T(8,128)(2,1)S(1)}, bf16[128,256]{1,0:T(8,128)(2,1)S(1)}, u32[]{:S(2)}, u32[]{:S(2)}) collective-permute-start(bf16[128,256]{1,0:T(8,128)(2,1)S(1)} %gather_fusion.12), channel_id=1, source_target_pairs={{0,1},{1,2},{2,3},{3,4},{4,5},{5,6},{6,7},{7,8},{8,9},{9,10},{10,1... | collective-permute-start | bytes 196616 | tf_op jit(solution)/shard_map/ppermute | solution.py:20
  602.5 652.4 %all-reduce.5.cloned.1.call-start = ((), (), s32[]{:S(2)}) async-start(), calls=%async_computation.1 | async-start | bytes 1048576 | tf_op jit(solution)/shard_map/psum | solution.py:218
  1255.6 44.1 %collective-permute-start.15 = (f32[3,256]{1,0:T(4,128)S(1)}, f32[3,256]{1,0:T(4,128)S(1)}, u32[]{:S(2)}, u32[]{:S(2)}) collective-permute-start(f32[3,256]{1,0:T(4,128)S(1)} %constant_dynamic-slice_fusion), channel_id=1, source_target_pairs={{0,128},{128,0},{1,129},{129,1},{2,130},{130,2},{3,131},{131,3},{4... | collective-permute-start | bytes 9224 | tf_op jit(solution)/shard_map/ppermute | solution.py:31
  (17 other events, 155.0 us)
Sparse Core Ops, SparseCore 0:
  602.7 91.3 all-reduce.2
  696.9 558.0 all-reduce.4
